TPU v7x, 256 devices: a whole 4x4x8 slice. The times are simulated.
256 devices in a mesh: seq: 32 (over z, y), exp: 4 (over x), dp: 2 (over core).
Axes of the slice: x: 4, y: 4, z: 8, core: 2. Of those that a mesh axis runs over, the one named last changes fastest.
Arguments:
- head_inputs: bfloat16 [16384, 4096], P(('dp', 'seq'), 'exp'), parts along dimension 0, may hold values from -6 to 6
- input_matrix: bfloat16 [16384, 128], P(('dp', 'seq')), parts along dimension 0, may hold values from -0.015625 to 0.015625
- output_matrix: bfloat16 [16384, 128], P(('dp', 'seq')), parts along dimension 0, may hold values from -6 to 6
- log_decay: float32 [64, 16384], P('exp', ('dp', 'seq')), parts along dimension 1, may hold values from -1 to 0
- skip_gain: float32 [64], P('exp'), may hold values from 0.5 to 1.5
- residual: bfloat16 [16384, 4096], P(('dp', 'seq', 'exp')), parts along dimension 0, may hold values from -6 to 6
- norm_gain: float32 [4096], replicated, may hold values from 0.1 to 1.9
- router_weight: bfloat16 [4096, 16], replicated, may hold values from -0.09375 to 0.09375
- expert_ids: int32 [16384, 2], P(('dp', 'seq', 'exp')), parts along dimension 0, may hold values from 0 to 15, as said below
- gate_weight: bfloat16 [4, 4096, 12288], P('exp', None, 'seq'), may hold values from -0.09375 to 0.09375
- up_weight: bfloat16 [4, 4096, 12288], P('exp', None, 'seq'), may hold values from -0.09375 to 0.09375
- down_weight: bfloat16 [4, 12288, 4096], P('exp', 'seq'), may hold values from -0.0546875 to 0.0546875
Outputs:
- layer_out: bfloat16 [16384, 4096], P(('dp', 'seq', 'exp')), parts along dimension 0
There are 2 independent parts, one for each index of `dp`. A program takes and returns all parts, laid end to end along the dimension named above; an argument that names none is the same for every part. Nothing has to cross between parts.
Inputs may be any that keep to these rules, and one draw needn't show every extreme that they name: `expert_ids`: each row names two different experts; the second column never names an expert below 4. In every aligned block of 64 rows each expert below 4 is named by at most 8 rows, and in every run of 4 consecutive blocks, starting at block 0, by at most 16 rows; in every run one such expert is named by exactly 8 rows in one block and by exactly 16 rows in the whole run.
All inputs are finite; a program needn't handle non-finite values.
Results may differ from a plain program's by a relative error of at most 0.015.
Values may be sent and summed in bfloat16 or wider, within the bound.
A program may use at most 128 MiB of HBM per device.

v0:
```python
import jax
import jax.numpy as jnp
from jax import lax
from jax.sharding import PartitionSpec as P

P_SIZE = 64
CAP = 8


def shifted(block, axis, distance):
    devices = range(lax.axis_size(axis))
    route = [(i - distance, i) for i in devices if i - distance in devices]
    return lax.ppermute(block, axis, route)


def body(
    head_inputs,
    input_matrix,
    output_matrix,
    log_decay,
    skip_gain,
    residual,
    norm_gain,
    router_weight,
    expert_ids,
    gate_weight,
    up_weight,
    down_weight,
):
    length = head_inputs.shape[0]
    heads = log_decay.shape[0]
    per_head = head_inputs.reshape(length, heads, P_SIZE)
    cumulative = jnp.cumsum(log_decay, axis=1)
    scores = jnp.dot(output_matrix, input_matrix.T, preferred_element_type=jnp.float32)
    causal = lax.broadcasted_iota(jnp.int32, (length, length), 0) >= lax.broadcasted_iota(
        jnp.int32, (length, length), 1
    )
    spread = jnp.minimum(cumulative[:, :, None] - cumulative[:, None, :], 0.0)
    mixing = jnp.where(causal[None], jnp.exp(spread) * scores[None], 0.0).astype(jnp.bfloat16)
    within = jnp.einsum("hts,shp->thp", mixing, per_head, preferred_element_type=jnp.float32)
    remain = jnp.exp(cumulative[:, -1:] - cumulative)
    weighted = (remain[:, :, None] * input_matrix.astype(jnp.float32)[None]).astype(jnp.bfloat16)
    local_state = jnp.einsum("shp,hsn->hpn", per_head, weighted, preferred_element_type=jnp.float32)
    block_decay = jnp.exp(cumulative[:, -1])

    def advance(iteration, incoming):
        outgoing = block_decay[:, None, None] * incoming + local_state
        return shifted(outgoing.astype(jnp.bfloat16), "seq", 1).astype(outgoing.dtype)

    entering = lax.fori_loop(0, lax.axis_size("seq") - 1, advance, jnp.zeros_like(local_state))
    carried = jnp.einsum(
        "tn,hpn->thp", output_matrix.astype(jnp.float32), entering, precision=lax.Precision.HIGHEST
    )
    carried = carried * jnp.exp(cumulative).T[:, :, None]
    mixed = within + carried + skip_gain[None, :, None] * per_head.astype(jnp.float32)
    mamba_out = mixed.reshape(length, heads * P_SIZE).astype(jnp.bfloat16)
    token_rows = lax.all_to_all(mamba_out, "exp", split_axis=0, concat_axis=1, tiled=True)
    stream = (residual.astype(jnp.float32) + token_rows.astype(jnp.float32)).astype(jnp.bfloat16)
    stream_wide = stream.astype(jnp.float32)
    normed = (
        stream_wide
        * lax.rsqrt(jnp.mean(stream_wide * stream_wide, axis=-1, keepdims=True) + 1e-06)
        * norm_gain
    ).astype(jnp.bfloat16)
    logits = jnp.dot(normed, router_weight, preferred_element_type=jnp.float32)
    expert_iota = lax.broadcasted_iota(jnp.int32, logits.shape, 1)
    first = expert_ids[:, 0]
    second = expert_ids[:, 1]
    first_logit = jnp.sum(jnp.where(expert_iota == first[:, None], logits, 0.0), axis=-1)
    second_logit = jnp.sum(jnp.where(expert_iota == second[:, None], logits, 0.0), axis=-1)
    gate = jax.nn.sigmoid(first_logit - second_logit)
    flight = lax.axis_size("exp")
    member = (first[:, None] == jnp.arange(flight, dtype=jnp.int32)[None, :]).astype(jnp.int32)
    ranking = jnp.cumsum(member, axis=0) - member
    slots = jnp.sum(ranking * member, axis=-1)
    chosen = (member.T[:, None, :] == 1) & (
        slots[None, None, :] == jnp.arange(CAP, dtype=jnp.int32)[None, :, None]
    )
    select = chosen.astype(jnp.bfloat16)
    outbound = jnp.einsum("ecr,rd->ecd", select, normed, preferred_element_type=jnp.float32).astype(
        jnp.bfloat16
    )
    model_width = outbound.shape[2]
    inbound = lax.all_to_all(outbound, "exp", split_axis=0, concat_axis=0, tiled=True)
    routed = inbound.reshape(flight * CAP, model_width)
    gate_part = gate_weight[0]
    up_part = up_weight[0]
    down_part = down_weight[0]
    fragment = lax.all_gather(routed, "seq", axis=0, tiled=True)
    gated = jnp.dot(fragment, gate_part, preferred_element_type=jnp.float32)
    lifted = jnp.dot(fragment, up_part, preferred_element_type=jnp.float32)
    hidden_all = (jax.nn.silu(gated) * lifted).astype(jnp.bfloat16)
    fragment = hidden_all
    summed = lax.psum_scatter(
        jnp.dot(fragment, down_part, preferred_element_type=jnp.float32).astype(jnp.bfloat16),
        "seq",
        scatter_dimension=0,
        tiled=True,
    )
    expert_out = summed.reshape(flight, CAP, model_width)
    returned = lax.all_to_all(expert_out, "exp", split_axis=0, concat_axis=0, tiled=True)
    combined = jnp.einsum("ecr,ecd->rd", select, returned, preferred_element_type=jnp.float32)
    return (stream_wide + gate[:, None] * combined).astype(jnp.bfloat16)


def solution(mesh):
    return jax.shard_map(
        body,
        mesh=mesh,
        in_specs=(
            P(("dp", "seq"), "exp"),
            P(("dp", "seq"), None),
            P(("dp", "seq"), None),
            P("exp", ("dp", "seq")),
            P("exp"),
            P(("dp", "seq", "exp"), None),
            P(),
            P(),
            P(("dp", "seq", "exp"), None),
            P("exp", None, "seq"),
            P("exp", None, "seq"),
            P("exp", "seq", None),
        ),
        out_specs=P(("dp", "seq", "exp"), None),
        check_vma=False,
    )
```

profile of v0, /device:TPU:4, one launch (start us, length us, event | category | flops | bytes accessed | tf_op | source)
XLA Modules:
  0.0 887.5 jit_solution(8230713345053279905)
XLA Ops:
  20.3 423.7 %while.11 = (s32[]{:T(128)}, f32[16,64,128]{2,1,0:T(8,128)}, f32[16]{0:T(128)S(1)}, f32[16,64,128]{2,1,0:T(8,128)}, s32[]{:T(128)}, /*index=5*/s32[]{:T(128)}) while((s32[]{:T(128)}, f32[16,64,128]{2,1,0:T(8,128)}, f32[16]{0:T(128)S(1)}, f32[16,64,128]{2,1,0:T(8,128)}, s32[]{:T(128)}, /*index=5*/s32[]{:T(128)}) %tuple.33), condition=%wide.region_3.4_spmd.clone, body=%wide.region_2.3_spmd.clone.sunk | while | flops 655363 | bytes 3145911 | solution.py:50
  93.7 6.4 collective-permute-start
  107.2 6.4 collective-permute-start
  120.7 6.4 collective-permute-start
  134.1 6.4 collective-permute-start
  148.1 6.7 collective-permute-start
  163.5 7.2 collective-permute-start
  170.7 6.9 collective-permute-done
  180.6 6.8 collective-permute-start
  196.1 6.1 collective-permute-start
  222.5 6.4 collective-permute-start
  236.0 6.4 collective-permute-start
  249.4 6.4 collective-permute-start
  262.9 6.4 collective-permute-start
  276.4 6.4 collective-permute-start
  289.9 6.4 collective-permute-start
  303.4 6.6 collective-permute-start
  318.1 7.0 collective-permute-start
  325.1 6.4 collective-permute-done
  334.4 7.3 collective-permute-start
  341.7 6.5 collective-permute-done
  351.0 6.7 collective-permute-start
  378.6 6.4 collective-permute-start
  392.1 6.4 collective-permute-start
  405.6 6.4 collective-permute-start
  419.1 6.4 collective-permute-start
  432.5 6.4 collective-permute-start
  464.7 10.0 %all_to_all.20 = bf16[4,8,4096]{2,1,0:T(8,128)(2,1)} all-to-all(bf16[4,8,4096]{2,1,0:T(8,128)(2,1)S(1)} %convolution_convert_fusion.1), channel_id=1, replica_groups=mesh['seq'=32,'exp'=4,'dp'=2] {'exp'}, dimensions={0} | all-to-all | bytes 524288 | tf_op jit(solution)/shard_map/all_to_all | solution.py:84
  474.7 148.3 %all-gather.2.cloned.1.call-done = bf16[1024,4096]{1,0:T(8,128)(2,1)} async-done(((bf16[32,4096]{1,0:T(8,128)(2,1)}), bf16[1024,4096]{1,0:T(8,128)(2,1)}) %all-gather.2.cloned.1.call-update) | async-done | bytes 8388624 | tf_op jit(solution)/shard_map/all_gather | solution.py:89
  623.1 8.0 fusion.8
  635.6 6.7 convolution_convert_fusion
  644.6 225.4 %reduce-scatter.2.cloned.1.call-done = bf16[32,4096]{1,0:T(8,128)(2,1)} async-done(((bf16[1024,4096]{1,0:T(8,128)(2,1)}), bf16[32,4096]{1,0:T(8,128)(2,1)}) %reduce-scatter.2.cloned.1.call-update) | async-done | bytes 262160 | tf_op jit(solution)/shard_map/reduce_scatter | solution.py:94
  (164 shorter events, 305.4 us)
Async XLA Ops:
  22.2 9.3 %collective-permute-start = (bf16[16,64,128]{2,1,0:T(8,128)(2,1)}, bf16[16,64,128]{2,1,0:T(8,128)(2,1)S(1)}, u32[]{:S(2)}, u32[]{:S(2)}) collective-permute-start(bf16[16,64,128]{2,1,0:T(8,128)(2,1)} %fusion.54), channel_id=1, source_target_pairs={{0,8},{8,16},{16,24},{24,32},{32,40},{40,48},{48,56},{56,64},{64,7... | collective-permute-start | bytes 786440 | tf_op jit(solution)/shard_map/while/body/eval_jaxpr/ppermute | solution.py:13
  34.5 9.3 %collective-permute-start = (bf16[16,64,128]{2,1,0:T(8,128)(2,1)}, bf16[16,64,128]{2,1,0:T(8,128)(2,1)S(1)}, u32[]{:S(2)}, u32[]{:S(2)}) collective-permute-start(bf16[16,64,128]{2,1,0:T(8,128)(2,1)} %fusion.54), channel_id=1, source_target_pairs={{0,8},{8,16},{16,24},{24,32},{32,40},{40,48},{48,56},{56,64},{64,7... | collective-permute-start | bytes 786440 | tf_op jit(solution)/shard_map/while/body/eval_jaxpr/ppermute | solution.py:13
  80.8 10.0 %collective-permute-start = (bf16[16,64,128]{2,1,0:T(8,128)(2,1)}, bf16[16,64,128]{2,1,0:T(8,128)(2,1)S(1)}, u32[]{:S(2)}, u32[]{:S(2)}) collective-permute-start(bf16[16,64,128]{2,1,0:T(8,128)(2,1)} %fusion.54), channel_id=1, source_target_pairs={{0,8},{8,16},{16,24},{24,32},{32,40},{40,48},{48,56},{56,64},{64,7... | collective-permute-start | bytes 786440 | tf_op jit(solution)/shard_map/while/body/eval_jaxpr/ppermute | solution.py:13
  93.7 10.6 %collective-permute-start = (bf16[16,64,128]{2,1,0:T(8,128)(2,1)}, bf16[16,64,128]{2,1,0:T(8,128)(2,1)S(1)}, u32[]{:S(2)}, u32[]{:S(2)}) collective-permute-start(bf16[16,64,128]{2,1,0:T(8,128)(2,1)} %fusion.54), channel_id=1, source_target_pairs={{0,8},{8,16},{16,24},{24,32},{32,40},{40,48},{48,56},{56,64},{64,7... | collective-permute-start | bytes 786440 | tf_op jit(solution)/shard_map/while/body/eval_jaxpr/ppermute | solution.py:13
  107.2 10.6 %collective-permute-start = (bf16[16,64,128]{2,1,0:T(8,128)(2,1)}, bf16[16,64,128]{2,1,0:T(8,128)(2,1)S(1)}, u32[]{:S(2)}, u32[]{:S(2)}) collective-permute-start(bf16[16,64,128]{2,1,0:T(8,128)(2,1)} %fusion.54), channel_id=1, source_target_pairs={{0,8},{8,16},{16,24},{24,32},{32,40},{40,48},{48,56},{56,64},{64,7... | collective-permute-start | bytes 786440 | tf_op jit(solution)/shard_map/while/body/eval_jaxpr/ppermute | solution.py:13
  120.7 10.6 %collective-permute-start = (bf16[16,64,128]{2,1,0:T(8,128)(2,1)}, bf16[16,64,128]{2,1,0:T(8,128)(2,1)S(1)}, u32[]{:S(2)}, u32[]{:S(2)}) collective-permute-start(bf16[16,64,128]{2,1,0:T(8,128)(2,1)} %fusion.54), channel_id=1, source_target_pairs={{0,8},{8,16},{16,24},{24,32},{32,40},{40,48},{48,56},{56,64},{64,7... | collective-permute-start | bytes 786440 | tf_op jit(solution)/shard_map/while/body/eval_jaxpr/ppermute | solution.py:13
  134.1 11.1 %collective-permute-start = (bf16[16,64,128]{2,1,0:T(8,128)(2,1)}, bf16[16,64,128]{2,1,0:T(8,128)(2,1)S(1)}, u32[]{:S(2)}, u32[]{:S(2)}) collective-permute-start(bf16[16,64,128]{2,1,0:T(8,128)(2,1)} %fusion.54), channel_id=1, source_target_pairs={{0,8},{8,16},{16,24},{24,32},{32,40},{40,48},{48,56},{56,64},{64,7... | collective-permute-start | bytes 786440 | tf_op jit(solution)/shard_map/while/body/eval_jaxpr/ppermute | solution.py:13
  148.1 12.5 %collective-permute-start = (bf16[16,64,128]{2,1,0:T(8,128)(2,1)}, bf16[16,64,128]{2,1,0:T(8,128)(2,1)S(1)}, u32[]{:S(2)}, u32[]{:S(2)}) collective-permute-start(bf16[16,64,128]{2,1,0:T(8,128)(2,1)} %fusion.54), channel_id=1, source_target_pairs={{0,8},{8,16},{16,24},{24,32},{32,40},{40,48},{48,56},{56,64},{64,7... | collective-permute-start | bytes 786440 | tf_op jit(solution)/shard_map/while/body/eval_jaxpr/ppermute | solution.py:13
  163.5 14.1 %collective-permute-start = (bf16[16,64,128]{2,1,0:T(8,128)(2,1)}, bf16[16,64,128]{2,1,0:T(8,128)(2,1)S(1)}, u32[]{:S(2)}, u32[]{:S(2)}) collective-permute-start(bf16[16,64,128]{2,1,0:T(8,128)(2,1)} %fusion.54), channel_id=1, source_target_pairs={{0,8},{8,16},{16,24},{24,32},{32,40},{40,48},{48,56},{56,64},{64,7... | collective-permute-start | bytes 786440 | tf_op jit(solution)/shard_map/while/body/eval_jaxpr/ppermute | solution.py:13
  180.6 12.6 %collective-permute-start = (bf16[16,64,128]{2,1,0:T(8,128)(2,1)}, bf16[16,64,128]{2,1,0:T(8,128)(2,1)S(1)}, u32[]{:S(2)}, u32[]{:S(2)}) collective-permute-start(bf16[16,64,128]{2,1,0:T(8,128)(2,1)} %fusion.54), channel_id=1, source_target_pairs={{0,8},{8,16},{16,24},{24,32},{32,40},{40,48},{48,56},{56,64},{64,7... | collective-permute-start | bytes 786440 | tf_op jit(solution)/shard_map/while/body/eval_jaxpr/ppermute | solution.py:13
  196.1 10.8 %collective-permute-start = (bf16[16,64,128]{2,1,0:T(8,128)(2,1)}, bf16[16,64,128]{2,1,0:T(8,128)(2,1)S(1)}, u32[]{:S(2)}, u32[]{:S(2)}) collective-permute-start(bf16[16,64,128]{2,1,0:T(8,128)(2,1)} %fusion.54), channel_id=1, source_target_pairs={{0,8},{8,16},{16,24},{24,32},{32,40},{40,48},{48,56},{56,64},{64,7... | collective-permute-start | bytes 786440 | tf_op jit(solution)/shard_map/while/body/eval_jaxpr/ppermute | solution.py:13
  209.9 9.7 %collective-permute-start = (bf16[16,64,128]{2,1,0:T(8,128)(2,1)}, bf16[16,64,128]{2,1,0:T(8,128)(2,1)S(1)}, u32[]{:S(2)}, u32[]{:S(2)}) collective-permute-start(bf16[16,64,128]{2,1,0:T(8,128)(2,1)} %fusion.54), channel_id=1, source_target_pairs={{0,8},{8,16},{16,24},{24,32},{32,40},{40,48},{48,56},{56,64},{64,7... | collective-permute-start | bytes 786440 | tf_op jit(solution)/shard_map/while/body/eval_jaxpr/ppermute | solution.py:13
  222.5 10.6 %collective-permute-start = (bf16[16,64,128]{2,1,0:T(8,128)(2,1)}, bf16[16,64,128]{2,1,0:T(8,128)(2,1)S(1)}, u32[]{:S(2)}, u32[]{:S(2)}) collective-permute-start(bf16[16,64,128]{2,1,0:T(8,128)(2,1)} %fusion.54), channel_id=1, source_target_pairs={{0,8},{8,16},{16,24},{24,32},{32,40},{40,48},{48,56},{56,64},{64,7... | collective-permute-start | bytes 786440 | tf_op jit(solution)/shard_map/while/body/eval_jaxpr/ppermute | solution.py:13
  236.0 10.6 %collective-permute-start = (bf16[16,64,128]{2,1,0:T(8,128)(2,1)}, bf16[16,64,128]{2,1,0:T(8,128)(2,1)S(1)}, u32[]{:S(2)}, u32[]{:S(2)}) collective-permute-start(bf16[16,64,128]{2,1,0:T(8,128)(2,1)} %fusion.54), channel_id=1, source_target_pairs={{0,8},{8,16},{16,24},{24,32},{32,40},{40,48},{48,56},{56,64},{64,7... | collective-permute-start | bytes 786440 | tf_op jit(solution)/shard_map/while/body/eval_jaxpr/ppermute | solution.py:13
  249.4 10.6 %collective-permute-start = (bf16[16,64,128]{2,1,0:T(8,128)(2,1)}, bf16[16,64,128]{2,1,0:T(8,128)(2,1)S(1)}, u32[]{:S(2)}, u32[]{:S(2)}) collective-permute-start(bf16[16,64,128]{2,1,0:T(8,128)(2,1)} %fusion.54), channel_id=1, source_target_pairs={{0,8},{8,16},{16,24},{24,32},{32,40},{40,48},{48,56},{56,64},{64,7... | collective-permute-start | bytes 786440 | tf_op jit(solution)/shard_map/while/body/eval_jaxpr/ppermute | solution.py:13
  262.9 10.6 %collective-permute-start = (bf16[16,64,128]{2,1,0:T(8,128)(2,1)}, bf16[16,64,128]{2,1,0:T(8,128)(2,1)S(1)}, u32[]{:S(2)}, u32[]{:S(2)}) collective-permute-start(bf16[16,64,128]{2,1,0:T(8,128)(2,1)} %fusion.54), channel_id=1, source_target_pairs={{0,8},{8,16},{16,24},{24,32},{32,40},{40,48},{48,56},{56,64},{64,7... | collective-permute-start | bytes 786440 | tf_op jit(solution)/shard_map/while/body/eval_jaxpr/ppermute | solution.py:13
  276.4 10.6 %collective-permute-start = (bf16[16,64,128]{2,1,0:T(8,128)(2,1)}, bf16[16,64,128]{2,1,0:T(8,128)(2,1)S(1)}, u32[]{:S(2)}, u32[]{:S(2)}) collective-permute-start(bf16[16,64,128]{2,1,0:T(8,128)(2,1)} %fusion.54), channel_id=1, source_target_pairs={{0,8},{8,16},{16,24},{24,32},{32,40},{40,48},{48,56},{56,64},{64,7... | collective-permute-start | bytes 786440 | tf_op jit(solution)/shard_map/while/body/eval_jaxpr/ppermute | solution.py:13
  289.9 10.6 %collective-permute-start = (bf16[16,64,128]{2,1,0:T(8,128)(2,1)}, bf16[16,64,128]{2,1,0:T(8,128)(2,1)S(1)}, u32[]{:S(2)}, u32[]{:S(2)}) collective-permute-start(bf16[16,64,128]{2,1,0:T(8,128)(2,1)} %fusion.54), channel_id=1, source_target_pairs={{0,8},{8,16},{16,24},{24,32},{32,40},{40,48},{48,56},{56,64},{64,7... | collective-permute-start | bytes 786440 | tf_op jit(solution)/shard_map/while/body/eval_jaxpr/ppermute | solution.py:13
  303.4 11.8 %collective-permute-start = (bf16[16,64,128]{2,1,0:T(8,128)(2,1)}, bf16[16,64,128]{2,1,0:T(8,128)(2,1)S(1)}, u32[]{:S(2)}, u32[]{:S(2)}) collective-permute-start(bf16[16,64,128]{2,1,0:T(8,128)(2,1)} %fusion.54), channel_id=1, source_target_pairs={{0,8},{8,16},{16,24},{24,32},{32,40},{40,48},{48,56},{56,64},{64,7... | collective-permute-start | bytes 786440 | tf_op jit(solution)/shard_map/while/body/eval_jaxpr/ppermute | solution.py:13
  318.1 13.4 %collective-permute-start = (bf16[16,64,128]{2,1,0:T(8,128)(2,1)}, bf16[16,64,128]{2,1,0:T(8,128)(2,1)S(1)}, u32[]{:S(2)}, u32[]{:S(2)}) collective-permute-start(bf16[16,64,128]{2,1,0:T(8,128)(2,1)} %fusion.54), channel_id=1, source_target_pairs={{0,8},{8,16},{16,24},{24,32},{32,40},{40,48},{48,56},{56,64},{64,7... | collective-permute-start | bytes 786440 | tf_op jit(solution)/shard_map/while/body/eval_jaxpr/ppermute | solution.py:13
  334.4 13.7 %collective-permute-start = (bf16[16,64,128]{2,1,0:T(8,128)(2,1)}, bf16[16,64,128]{2,1,0:T(8,128)(2,1)S(1)}, u32[]{:S(2)}, u32[]{:S(2)}) collective-permute-start(bf16[16,64,128]{2,1,0:T(8,128)(2,1)} %fusion.54), channel_id=1, source_target_pairs={{0,8},{8,16},{16,24},{24,32},{32,40},{40,48},{48,56},{56,64},{64,7... | collective-permute-start | bytes 786440 | tf_op jit(solution)/shard_map/while/body/eval_jaxpr/ppermute | solution.py:13
  351.0 12.0 %collective-permute-start = (bf16[16,64,128]{2,1,0:T(8,128)(2,1)}, bf16[16,64,128]{2,1,0:T(8,128)(2,1)S(1)}, u32[]{:S(2)}, u32[]{:S(2)}) collective-permute-start(bf16[16,64,128]{2,1,0:T(8,128)(2,1)} %fusion.54), channel_id=1, source_target_pairs={{0,8},{8,16},{16,24},{24,32},{32,40},{40,48},{48,56},{56,64},{64,7... | collective-permute-start | bytes 786440 | tf_op jit(solution)/shard_map/while/body/eval_jaxpr/ppermute | solution.py:13
  366.0 9.7 %collective-permute-start = (bf16[16,64,128]{2,1,0:T(8,128)(2,1)}, bf16[16,64,128]{2,1,0:T(8,128)(2,1)S(1)}, u32[]{:S(2)}, u32[]{:S(2)}) collective-permute-start(bf16[16,64,128]{2,1,0:T(8,128)(2,1)} %fusion.54), channel_id=1, source_target_pairs={{0,8},{8,16},{16,24},{24,32},{32,40},{40,48},{48,56},{56,64},{64,7... | collective-permute-start | bytes 786440 | tf_op jit(solution)/shard_map/while/body/eval_jaxpr/ppermute | solution.py:13
  378.6 10.6 %collective-permute-start = (bf16[16,64,128]{2,1,0:T(8,128)(2,1)}, bf16[16,64,128]{2,1,0:T(8,128)(2,1)S(1)}, u32[]{:S(2)}, u32[]{:S(2)}) collective-permute-start(bf16[16,64,128]{2,1,0:T(8,128)(2,1)} %fusion.54), channel_id=1, source_target_pairs={{0,8},{8,16},{16,24},{24,32},{32,40},{40,48},{48,56},{56,64},{64,7... | collective-permute-start | bytes 786440 | tf_op jit(solution)/shard_map/while/body/eval_jaxpr/ppermute | solution.py:13
  392.1 10.6 %collective-permute-start = (bf16[16,64,128]{2,1,0:T(8,128)(2,1)}, bf16[16,64,128]{2,1,0:T(8,128)(2,1)S(1)}, u32[]{:S(2)}, u32[]{:S(2)}) collective-permute-start(bf16[16,64,128]{2,1,0:T(8,128)(2,1)} %fusion.54), channel_id=1, source_target_pairs={{0,8},{8,16},{16,24},{24,32},{32,40},{40,48},{48,56},{56,64},{64,7... | collective-permute-start | bytes 786440 | tf_op jit(solution)/shard_map/while/body/eval_jaxpr/ppermute | solution.py:13
  405.6 10.6 %collective-permute-start = (bf16[16,64,128]{2,1,0:T(8,128)(2,1)}, bf16[16,64,128]{2,1,0:T(8,128)(2,1)S(1)}, u32[]{:S(2)}, u32[]{:S(2)}) collective-permute-start(bf16[16,64,128]{2,1,0:T(8,128)(2,1)} %fusion.54), channel_id=1, source_target_pairs={{0,8},{8,16},{16,24},{24,32},{32,40},{40,48},{48,56},{56,64},{64,7... | collective-permute-start | bytes 786440 | tf_op jit(solution)/shard_map/while/body/eval_jaxpr/ppermute | solution.py:13
  419.1 10.6 %collective-permute-start = (bf16[16,64,128]{2,1,0:T(8,128)(2,1)}, bf16[16,64,128]{2,1,0:T(8,128)(2,1)S(1)}, u32[]{:S(2)}, u32[]{:S(2)}) collective-permute-start(bf16[16,64,128]{2,1,0:T(8,128)(2,1)} %fusion.54), channel_id=1, source_target_pairs={{0,8},{8,16},{16,24},{24,32},{32,40},{40,48},{48,56},{56,64},{64,7... | collective-permute-start | bytes 786440 | tf_op jit(solution)/shard_map/while/body/eval_jaxpr/ppermute | solution.py:13
  432.5 10.6 %collective-permute-start = (bf16[16,64,128]{2,1,0:T(8,128)(2,1)}, bf16[16,64,128]{2,1,0:T(8,128)(2,1)S(1)}, u32[]{:S(2)}, u32[]{:S(2)}) collective-permute-start(bf16[16,64,128]{2,1,0:T(8,128)(2,1)} %fusion.54), channel_id=1, source_target_pairs={{0,8},{8,16},{16,24},{24,32},{32,40},{40,48},{48,56},{56,64},{64,7... | collective-permute-start | bytes 786440 | tf_op jit(solution)/shard_map/while/body/eval_jaxpr/ppermute | solution.py:13
  452.0 10.0 %all-to-all-start = ((bf16[4,64,1024]{2,1,0:T(8,128)(2,1)}), bf16[4,64,1024]{2,1,0:T(8,128)(2,1)}, u32[]{:S(2)}, u32[]{:S(2)}) async-start(bf16[4,64,1024]{2,1,0:T(8,128)(2,1)} %copy.30), calls=%async_computation | async-start | bytes 1048576 | tf_op jit(solution)/shard_map/all_to_all | solution.py:57
  456.8 166.3 %all-gather.2.cloned.1.call-start = ((), (), s32[]{:S(2)}) async-start(), calls=%async_computation.4 | async-start | bytes 8650752 | tf_op jit(solution)/shard_map/all_gather | solution.py:89
  474.7 395.3 %reduce-scatter.2.cloned.1.call-start = ((), (), s32[]{:S(2)}) async-start(), calls=%async_computation.5 | async-start | bytes 8650752 | tf_op jit(solution)/shard_map/reduce_scatter | solution.py:94
  870.0 8.5 all-to-all-start.2
  (15 other events, 1546.0 us)
Sparse Core Ops, SparseCore 0:
  474.8 148.1 all-gather.1
  642.5 227.4 reduce-scatter.1
where the time goes:
time: 891 us; the launch traced here: 887 us
  waiting for transfers between devices  528 us (59%)
  starting transfers between devices  197 us (22%)
  other arithmetic  94.8 us (11%)
  matrix products  33.1 us (4%)
  between operations  13.6 us (2%)
  local copies, waits for them, and re-layouts  10.6 us (1%)
  blocking collectives  10 us (1%)
    reduce_scatter x1, waiting for transfers between devices, body(): lax.psum_scatter(jnp.dot(fragment, down_part, preferred_element_type=jnp....  225 us
    ppermute x31, starting transfers between devices, shifted(): return lax.ppermute(block, axis, route)  188 us
    all_gather x1, waiting for transfers between devices, body(): fragment = lax.all_gather(routed, 'seq', axis=0, tiled=True)  148 us
    ppermute x31, waiting for transfers between devices, shifted(): return lax.ppermute(block, axis, route)  146 us
    convert_element_type x31, other arithmetic, advance(): outgoing.astype(jnp.bfloat16)  63.5 us
    convert_element_type x31, other arithmetic, advance(): shifted(outgoing.astype(jnp.bfloat16), 'seq', 1).astype(outgoing.dtype)  26.7 us
  transfers between devices with their start and end apart: 35, of which 35 were waited for; matrix products, arithmetic and copies ran while one was open for 0% of the time, Pallas kernels for 0%

commit v1 on v0

v1 whole, which is shorter than its diff:
```python
import functools

import jax
import jax.numpy as jnp
from jax import lax
from jax.experimental import pallas as pl
from jax.experimental.pallas import tpu as pltpu
from jax.sharding import PartitionSpec as P

MESH = pl.DeviceIdType.MESH
BF16 = jnp.bfloat16
F32 = jnp.float32
HIGH = lax.Precision.HIGHEST
P_SIZE = 64
CAP = 8
ROWS = 64
RUN_CAP = 16
NX = 4
NY = 4
NZ = 8
SEQ = NY * NZ
CONTRACT_ROWS = (((0,), (0,)), ((), ()))
CONTRACT_COLS = (((1,), (1,)), ((), ()))


def iota(shape, axis):
    return lax.broadcasted_iota(jnp.int32, shape, axis)


def block_select(first_row, experts, slots_each):
    shape = (experts * slots_each, ROWS)
    row_expert = iota(shape, 0) // slots_each
    member = (first_row == row_expert).astype(F32)
    before = (iota((ROWS, ROWS), 0) < iota((ROWS, ROWS), 1)).astype(BF16)
    rank = jnp.dot(member.astype(BF16), before, preferred_element_type=F32)
    count = jnp.sum(member, axis=1, keepdims=True)
    return member, rank, count


def mamba_kernel(
    decay_ref, x_ref, b_ref, c_ref, skip_ref, residual_ref, ids_ref,
    out_ref, picked_ref, ids_out_ref,
    dec_send, dec_recv, s_send, s_recv, e_send, e_recv, acc, grow, r_send, r_recv, ids_all,
    sems, x_send_sems,
):
    me = lax.axis_index("seq")
    mx = lax.axis_index("exp")
    length = x_ref.shape[0]
    heads = decay_ref.shape[0]

    def seq_peer(i):
        q = i // NY
        dz = NZ // 2 + ((q + 1) // 2) * (1 - 2 * (q % 2))
        dy = NY - 1 - i % NY
        z = (me // NY + dz) % NZ
        y = (me % NY + dy) % NY
        return z * NY + y

    barrier = pltpu.get_barrier_semaphore()

    def greet(i, carry):
        pl.semaphore_signal(barrier, inc=1, device_id={"seq": seq_peer(i)}, device_id_type=MESH)
        return carry

    lax.fori_loop(0, SEQ - 1, greet, 0)
    for d in range(1, NX):
        pl.semaphore_signal(barrier, inc=1, device_id={"exp": (mx + d) % NX}, device_id_type=MESH)

    decay = decay_ref[...]
    upper = (iota((length, length), 0) <= iota((length, length), 1)).astype(F32)
    cum = jnp.dot(decay, upper, preferred_element_type=F32, precision=HIGH)
    lower = (iota((length, length), 0) >= iota((length, length), 1)).astype(F32)
    cum_t = lax.dot_general(lower, decay, CONTRACT_COLS, preferred_element_type=F32, precision=HIGH)
    total = jnp.exp(jnp.broadcast_to(cum[:, length - 1 : length], (heads, 128)))
    for h in range(heads):
        dec_send[h] = total[h : h + 1, :]
    left = iota((length, 2 * P_SIZE), 1) < P_SIZE

    def spread(columns, i):
        wide = (length, 2 * P_SIZE)
        a = jnp.broadcast_to(columns[:, 2 * i : 2 * i + 1], wide)
        b = jnp.broadcast_to(columns[:, 2 * i + 1 : 2 * i + 2], wide)
        return jnp.where(left, a, b)

    remain = jnp.exp(cum_t[length - 1 : length, :] - cum_t)
    for i in range(heads // 2):
        pair = slice(128 * i, 128 * i + 128)
        weighted = (x_ref[:, pair].astype(F32) * spread(remain, i)).astype(BF16)
        state = lax.dot_general(weighted, b_ref[...], CONTRACT_ROWS, preferred_element_type=F32)
        s_send[4 * i : 4 * i + 4] = state.astype(BF16).reshape(4, 32, 128)

    pl.semaphore_wait(barrier, SEQ - 1 + NX - 1)

    def scatter(i, carry):
        j = seq_peer(i)
        pltpu.make_async_remote_copy(
            src_ref=s_send.at[j], dst_ref=s_recv.at[me], send_sem=sems.at[0], recv_sem=sems.at[1],
            device_id={"seq": j}, device_id_type=MESH,
        ).start()
        pltpu.make_async_remote_copy(
            src_ref=dec_send.at[j // 2], dst_ref=dec_recv.at[me], send_sem=sems.at[2], recv_sem=sems.at[3],
            device_id={"seq": j}, device_id_type=MESH,
        ).start()
        return carry

    lax.fori_loop(0, SEQ - 1, scatter, 0)
    s_recv[me] = s_send[me]
    dec_recv[me] = dec_send[me // 2]

    ids = ids_ref[...]
    member, rank, _ = block_select(ids[0:1, :ROWS], NX, CAP)
    slot = (iota((NX * CAP, ROWS), 0) % CAP).astype(F32)
    select = jnp.where(rank == slot, member, 0.0).astype(BF16)
    rows = jnp.dot(select, residual_ref[...], preferred_element_type=F32)
    r_send[...] = rows.astype(BF16).reshape(NX, CAP, residual_ref.shape[1])
    for d in range(1, NX):
        to = (mx + d) % NX
        pltpu.make_async_remote_copy(
            src_ref=r_send.at[to], dst_ref=r_recv.at[mx], send_sem=x_send_sems.at[0], recv_sem=sems.at[6],
            device_id={"exp": to}, device_id_type=MESH,
        ).start()
        pltpu.make_async_remote_copy(
            src_ref=ids_ref, dst_ref=ids_all.at[mx], send_sem=x_send_sems.at[1], recv_sem=sems.at[7],
            device_id={"exp": to}, device_id_type=MESH,
        ).start()
    r_recv[mx] = r_send[mx]
    ids_all[mx] = ids

    scores = lax.dot_general(c_ref[...], b_ref[...], CONTRACT_COLS, preferred_element_type=F32)
    scores = jnp.where(iota(scores.shape, 0) >= iota(scores.shape, 1), scores, 0.0)
    grown = jnp.exp(cum_t)
    for i in range(heads // 2):
        pair = slice(128 * i, 128 * i + 128)
        x_pair = x_ref[:, pair]
        parts = []
        for h in (2 * i, 2 * i + 1):
            gap = jnp.minimum(cum_t[:, h : h + 1] - cum[h : h + 1, :], 0.0)
            mixing = (jnp.exp(gap) * scores).astype(BF16)
            parts.append(jnp.dot(mixing, x_pair, preferred_element_type=F32))
        own = jnp.where(left, parts[0], parts[1])
        acc[:, pair] = own + skip_ref[:, pair] * x_pair.astype(F32)
        grow[:, pair] = spread(grown, i)

    def drain(ref, sem):
        pltpu.make_async_copy(ref, ref, sem).wait()

    drain(dec_recv.at[pl.ds(0, SEQ - 1)], sems.at[3])
    drain(s_recv.at[pl.ds(0, SEQ - 1)], sems.at[1])
    entering = jnp.zeros((32, 128), F32)
    for k in range(SEQ):
        e_send[k] = entering.astype(BF16)
        if k < SEQ - 1:
            entering = entering * dec_recv[k] + s_recv[k].astype(F32)

    def gather(i, carry):
        j = seq_peer(i)
        pltpu.make_async_remote_copy(
            src_ref=e_send.at[j], dst_ref=e_recv.at[me], send_sem=sems.at[4], recv_sem=sems.at[5],
            device_id={"seq": j}, device_id_type=MESH,
        ).start()
        return carry

    lax.fori_loop(0, SEQ - 1, gather, 0)
    e_recv[me] = e_send[me]

    drain(r_recv.at[pl.ds(0, NX - 1)], sems.at[6])
    drain(ids_all.at[pl.ds(0, NX - 1)], sems.at[7])
    picked_ref[...] = r_recv[...].reshape(picked_ref.shape)
    ids_out_ref[...] = ids_all[...]

    drain(e_recv.at[pl.ds(0, SEQ - 1)], sems.at[5])
    for i in range(heads // 2):
        pair = slice(128 * i, 128 * i + 128)
        carried = lax.dot_general(
            c_ref[...], e_recv[4 * i : 4 * i + 4].reshape(128, 128), CONTRACT_COLS, preferred_element_type=F32
        )
        out_ref[:, pair] = (acc[:, pair] + grow[:, pair] * carried).astype(BF16)

    drain(s_send.at[pl.ds(0, SEQ - 1)], sems.at[0])
    drain(dec_recv.at[pl.ds(0, SEQ - 1)], sems.at[2])
    drain(e_send.at[pl.ds(0, SEQ - 1)], sems.at[4])
    drain(r_send.at[pl.ds(0, NX - 1)], x_send_sems.at[0])
    drain(ids_all.at[pl.ds(0, NX - 1)], x_send_sems.at[1])


def mamba(x, b, c, decay, skip_row, residual, ids_rows):
    length, width = x.shape
    heads = decay.shape[0]
    d = residual.shape[1]
    vmem = pl.BlockSpec(memory_space=pltpu.VMEM)
    return pl.pallas_call(
        mamba_kernel,
        out_shape=(
            jax.ShapeDtypeStruct((length, width), BF16),
            jax.ShapeDtypeStruct((NX * CAP, d), BF16),
            jax.ShapeDtypeStruct((NX, 8, 128), jnp.int32),
        ),
        in_specs=[vmem] * 7,
        out_specs=(vmem, vmem, vmem),
        scratch_shapes=[
            pltpu.VMEM((heads, 1, 128), F32),
            pltpu.VMEM((SEQ, 1, 128), F32),
            pltpu.VMEM((SEQ, 32, 128), BF16),
            pltpu.VMEM((SEQ, 32, 128), BF16),
            pltpu.VMEM((SEQ, 32, 128), BF16),
            pltpu.VMEM((SEQ, 32, 128), BF16),
            pltpu.VMEM((length, width), F32),
            pltpu.VMEM((length, width), F32),
            pltpu.VMEM((NX, CAP, d), BF16),
            pltpu.VMEM((NX, CAP, d), BF16),
            pltpu.VMEM((NX, 8, 128), jnp.int32),
            pltpu.SemaphoreType.DMA((8,)),
            pltpu.SemaphoreType.DMA((2,)),
        ],
        compiler_params=pltpu.CompilerParams(collective_id=0, has_side_effects=True),
        name="mamba",
    )(decay, x, b, c, skip_row, residual, ids_rows)


def body(
    head_inputs, input_matrix, output_matrix, log_decay, skip_gain, residual, norm_gain,
    router_weight, expert_ids, gate_weight, up_weight, down_weight,
):
    skip_row = jnp.repeat(skip_gain, P_SIZE)[None, :]
    ids_rows = jnp.pad(expert_ids.T, ((0, 6), (0, 64)), constant_values=99)
    mamba_out, picked, ids_all = mamba(
        head_inputs, input_matrix, output_matrix, log_decay, skip_row, residual, ids_rows
    )
    token_rows = lax.all_to_all(mamba_out, "exp", split_axis=0, concat_axis=1, tiled=True)
    stream = (residual.astype(jnp.float32) + token_rows.astype(jnp.float32)).astype(jnp.bfloat16)
    stream_wide = stream.astype(jnp.float32)
    normed = (
        stream_wide
        * lax.rsqrt(jnp.mean(stream_wide * stream_wide, axis=-1, keepdims=True) + 1e-06)
        * norm_gain
    ).astype(jnp.bfloat16)
    logits = jnp.dot(normed, router_weight, preferred_element_type=jnp.float32)
    expert_iota = lax.broadcasted_iota(jnp.int32, logits.shape, 1)
    first = expert_ids[:, 0]
    second = expert_ids[:, 1]
    first_logit = jnp.sum(jnp.where(expert_iota == first[:, None], logits, 0.0), axis=-1)
    second_logit = jnp.sum(jnp.where(expert_iota == second[:, None], logits, 0.0), axis=-1)
    gate = jax.nn.sigmoid(first_logit - second_logit)
    flight = lax.axis_size("exp")
    member = (first[:, None] == jnp.arange(flight, dtype=jnp.int32)[None, :]).astype(jnp.int32)
    ranking = jnp.cumsum(member, axis=0) - member
    slots = jnp.sum(ranking * member, axis=-1)
    chosen = (member.T[:, None, :] == 1) & (
        slots[None, None, :] == jnp.arange(CAP, dtype=jnp.int32)[None, :, None]
    )
    select = chosen.astype(jnp.bfloat16)
    outbound = jnp.einsum("ecr,rd->ecd", select, normed, preferred_element_type=jnp.float32).astype(
        jnp.bfloat16
    )
    model_width = outbound.shape[2]
    inbound = lax.all_to_all(outbound, "exp", split_axis=0, concat_axis=0, tiled=True)
    routed = inbound.reshape(flight * CAP, model_width)
    fragment = lax.all_gather(routed, "seq", axis=0, tiled=True)
    gated = jnp.dot(fragment, gate_weight[0], preferred_element_type=jnp.float32)
    lifted = jnp.dot(fragment, up_weight[0], preferred_element_type=jnp.float32)
    hidden_all = (jax.nn.silu(gated) * lifted).astype(jnp.bfloat16)
    summed = lax.psum_scatter(
        jnp.dot(hidden_all, down_weight[0], preferred_element_type=jnp.float32).astype(jnp.bfloat16),
        "seq",
        scatter_dimension=0,
        tiled=True,
    )
    expert_out = summed.reshape(flight, CAP, model_width)
    returned = lax.all_to_all(expert_out, "exp", split_axis=0, concat_axis=0, tiled=True)
    combined = jnp.einsum("ecr,ecd->rd", select, returned, preferred_element_type=jnp.float32)
    return (stream_wide + gate[:, None] * combined).astype(jnp.bfloat16)


def solution(mesh):
    return jax.shard_map(
        body,
        mesh=mesh,
        in_specs=(
            P(("dp", "seq"), "exp"),
            P(("dp", "seq"), None),
            P(("dp", "seq"), None),
            P("exp", ("dp", "seq")),
            P("exp"),
            P(("dp", "seq", "exp"), None),
            P(),
            P(),
            P(("dp", "seq", "exp"), None),
            P("exp", None, "seq"),
            P("exp", None, "seq"),
            P("exp", "seq", None),
        ),
        out_specs=P(("dp", "seq", "exp"), None),
        check_vma=False,
    )
```

time: 891 us -> 426 us (0.48)
  waiting for transfers between devices: 528 us -> 331 us
  starting transfers between devices: 197 us -> 9.65 us
  other arithmetic: 94.8 us -> 1.83 us
  Pallas kernels: 0 us -> 29 us
  matrix products: 33.1 us -> 23.1 us
    ppermute x31 -> x0, starting transfers between devices: 188 us -> none  [shifted(): return lax.ppermute(block, axis, route)]
    ppermute x31 -> x0, waiting for transfers between devices: 146 us -> none  [shifted(): return lax.ppermute(block, axis, route)]
    convert_element_type x63 -> x0, other arithmetic: 91 us -> none  [the longest x31 63.5 us: advance(): outgoing.astype(jnp.bfloat16)]
    all_gather x1, waiting for transfers between devices: 148 us -> 96 us  [body(): fragment = lax.all_gather(routed, 'seq', axis=0, tiled=True)]
    pallas_call x0 -> x1, Pallas kernels: none -> 29 us  [mamba(): pl.pallas_call(mamba_kernel, out_shape=(jax.ShapeDtypeStruct((length, wid...]
    dot_general x7 -> x3, matrix products: 29.2 us -> 19.2 us  [the longest x1 7.97 us: body(): jnp.dot(fragment, gate_weight[0], preferred_element_type=jnp.float32)]
  transfers between devices with their start and end apart: 35 -> 4, of which waited for: 35 -> 4; matrix products, arithmetic and copies ran while one was open for 0% -> 1% of each run, Pallas kernels for 0% -> 0%
where the time goes in v1:
time: 426 us; the launch traced here: 424 us
  waiting for transfers between devices  331 us (78%)
  Pallas kernels  29 us (7%)
  matrix products  23.1 us (5%)
  between operations  13.5 us (3%)
  blocking collectives  9.99 us (2%)
  starting transfers between devices  9.65 us (2%)
  local copies, waits for them, and re-layouts  5.33 us (1%)
    reduce_scatter x1, waiting for transfers between devices, body(): lax.psum_scatter(jnp.dot(hidden_all, down_weight[0], preferred_element_ty...  226 us
    all_gather x1, waiting for transfers between devices, body(): fragment = lax.all_gather(routed, 'seq', axis=0, tiled=True)  96 us
    pallas_call x1, Pallas kernels, mamba(): pl.pallas_call(mamba_kernel, out_shape=(jax.ShapeDtypeStruct((length, wid...  29 us
    all_to_all x1, blocking collectives, body(): lax.all_to_all(outbound, 'exp', split_axis=0, concat_axis=0, tiled=True)  9.99 us
  transfers between devices with their start and end apart: 4, of which 4 were waited for; matrix products, arithmetic and copies ran while one was open for 1% of the time, Pallas kernels for 0%

profile of v1, /device:TPU:4, one launch (start us, length us, event | category | flops | bytes accessed | tf_op | source)
XLA Modules:
  0.0 423.6 jit_solution(12445518024724909928)
XLA Ops:
  6.5 0.9 broadcast_in_dim.7
  7.4 0.7 broadcast_in_dim_reshape.3.skip_ref
  8.1 1.3 pad.4.ids_ref
  9.4 29.0 %mamba.1 = (bf16[256,1024]{1,0:T(8,128)(2,1)}, bf16[32,4096]{1,0:T(8,128)(2,1)}, s32[4,8,128]{2,1,0:T(8,128)}) custom-call(f32[16,256]{1,0:T(8,128)} %decay_ref.1, bf16[256,1024]{1,0:T(8,128)(2,1)} %x_ref.1, bf16[256,128]{1,0:T(8,128)(2,1)} %b_ref.1, bf16[256,128]{1,0:T(8,128)(2,1)} %c_ref.1, f32[1,1024]{1,0:T(1,128)} %broadcast_in_dim_reshape.3.skip_ref, ...), custom_call_target="tpu_custom_call" | custom-call | tf_op jit(solution)/shard_map/mamba/pallas_call | solution.py:191
  38.3 4.8 %all-to-all-start = ((bf16[4,64,1024]{2,1,0:T(8,128)(2,1)}), bf16[4,64,1024]{2,1,0:T(8,128)(2,1)}, u32[]{:S(2)}, u32[]{:S(2)}) async-start(bf16[4,64,1024]{2,1,0:T(8,128)(2,1)} %bitcast.41), calls=%async_computation | async-start | bytes 1048576 | tf_op jit(solution)/shard_map/all_to_all | solution.py:229
  43.2 0.8 slice_bitcast_fusion
  43.9 0.1 fusion.17
  44.0 0.1 reduce_window_sum.11
  44.1 0.2 select_reduce_fusion
  44.3 5.1 %all-to-all-done = bf16[4,64,1024]{2,1,0:T(8,128)(2,1)} async-done(((bf16[4,64,1024]{2,1,0:T(8,128)(2,1)}), bf16[4,64,1024]{2,1,0:T(8,128)(2,1)}, u32[]{:S(2)}, u32[]{:S(2)}) %all-to-all-start) | async-done | bytes 524320 | tf_op jit(solution)/shard_map/all_to_all | solution.py:229
  49.4 1.2 convert_bitcast_fusion
  50.6 0.1 copy.14
  50.7 0.0 copy-done.1
  50.7 0.3 fusion.10
  50.9 0.0 copy-start.2
  51.0 0.8 copy-done.2
  51.7 0.3 convolution_convert_fusion.1
  52.1 10.0 %all_to_all.23 = bf16[4,8,4096]{2,1,0:T(8,128)(2,1)} all-to-all(bf16[4,8,4096]{2,1,0:T(8,128)(2,1)S(1)} %convolution_convert_fusion.1), channel_id=1, replica_groups=mesh['seq'=32,'exp'=4,'dp'=2] {'exp'}, dimensions={0} | all-to-all | bytes 524288 | tf_op jit(solution)/shard_map/all_to_all | solution.py:256
  62.1 0.0 all-gather.2.cloned.1.call-update
  62.1 0.0 reduce-scatter.2.cloned.1.call-start
  62.1 96.0 %all-gather.2.cloned.1.call-done = bf16[1024,4096]{1,0:T(8,128)(2,1)} async-done(((bf16[32,4096]{1,0:T(8,128)(2,1)}), bf16[1024,4096]{1,0:T(8,128)(2,1)}) %all-gather.2.cloned.1.call-update) | async-done | bytes 8388624 | tf_op jit(solution)/shard_map/all_gather | solution.py:258
  158.1 8.0 %fusion.6 = f32[1024,384]{1,0:T(8,128)S(1)} fusion(bf16[1024,4096]{1,0:T(8,128)(2,1)} %all-gather.2.cloned.1.call-done, bf16[1,4096,384]{2,1,0:T(8,128)(2,1)} %param.21), kind=kOutput, calls=%fused_computation.9 | convolution fusion | flops 3221225472 | bytes 13107200 | tf_op jit(solution)/shard_map/dot_general | solution.py:259
  166.1 4.6 %multiply_convert_fusion = bf16[1024,384]{1,0:T(8,128)(2,1)S(1)} fusion(f32[1024,384]{1,0:T(8,128)S(1)} %fusion.6, bf16[1024,4096]{1,0:T(8,128)(2,1)S(1)} %copy-done.3, bf16[1,4096,384]{2,1,0:T(8,128)(2,1)S(1)} %copy-done.4), kind=kOutput, calls=%fused_computation.11 | convolution fusion | flops 3223584768 | bytes 13893632 | tf_op jit(solution)/shard_map/dot_general | solution.py:260
  170.7 0.0 copy-done
  170.7 6.7 %convolution_convert_fusion = bf16[1024,4096]{1,0:T(8,128)(2,1)} fusion(bf16[1024,384]{1,0:T(8,128)(2,1)S(1)} %multiply_convert_fusion, bf16[1,384,4096]{2,1,0:T(8,128)(2,1)S(1)} %copy-done), kind=kOutput, calls=%fused_computation | convolution fusion | flops 3225419776 | bytes 12320768 | tf_op jit(solution)/shard_map/dot_general | solution.py:263
  177.4 0.0 reduce-scatter.2.cloned.1.call-update
  177.4 0.9 copy-done.5
  178.3 1.4 select_reduce_fusion.1
  179.7 226.4 %reduce-scatter.2.cloned.1.call-done = bf16[32,4096]{1,0:T(8,128)(2,1)} async-done(((bf16[1024,4096]{1,0:T(8,128)(2,1)}), bf16[32,4096]{1,0:T(8,128)(2,1)}) %reduce-scatter.2.cloned.1.call-update) | async-done | bytes 262160 | tf_op jit(solution)/shard_map/reduce_scatter | solution.py:262
  406.1 4.8 %all-to-all-start.2 = ((bf16[4,8,4096]{2,1,0:T(8,128)(2,1)}), bf16[4,8,4096]{2,1,0:T(8,128)(2,1)S(1)}, u32[]{:S(2)}, u32[]{:S(2)}) async-start(bf16[4,8,4096]{2,1,0:T(8,128)(2,1)} %bitcast.42), calls=%async_computation.3 | async-start | bytes 524288 | tf_op jit(solution)/shard_map/all_to_all | solution.py:269
  410.9 3.7 all-to-all-done.2
  414.6 2.2 fusion.2
  (14 shorter events, 0.0 us)
Async XLA Ops:
  6.5 164.2 %copy-start = (bf16[1,384,4096]{2,1,0:T(8,128)(2,1)S(1)}, bf16[1,384,4096]{2,1,0:T(8,128)(2,1)}, u32[]{:S(2)}) copy-start(bf16[1,384,4096]{2,1,0:T(8,128)(2,1)} %param.23) | copy-start | bytes 9437188
  38.3 11.0 %all-to-all-start = ((bf16[4,64,1024]{2,1,0:T(8,128)(2,1)}), bf16[4,64,1024]{2,1,0:T(8,128)(2,1)}, u32[]{:S(2)}, u32[]{:S(2)}) async-start(bf16[4,64,1024]{2,1,0:T(8,128)(2,1)} %bitcast.41), calls=%async_computation | async-start | bytes 1048576 | tf_op jit(solution)/shard_map/all_to_all | solution.py:229
  43.2 8.6 %copy-start.6 = (f32[4096]{0:T(1024)S(1)}, f32[4096]{0:T(1024)}, u32[]{:S(2)}) copy-start(f32[4096]{0:T(1024)} %param.18) | copy-start | bytes 49156
  43.2 115.0 %all-gather.2.cloned.1.call-start = ((), (), s32[]{:S(2)}) async-start(), calls=%async_computation.4 | async-start | bytes 8650752 | tf_op jit(solution)/shard_map/all_gather | solution.py:258
  49.4 1.3 copy-start.1
  50.9 0.8 copy-start.2
  62.1 344.0 %reduce-scatter.2.cloned.1.call-start = ((), (), s32[]{:S(2)}) async-start(), calls=%async_computation.5 | async-start | bytes 8650752 | tf_op jit(solution)/shard_map/reduce_scatter | solution.py:262
  158.1 8.0 %copy-start.3 = (bf16[1024,4096]{1,0:T(8,128)(2,1)S(1)}, bf16[1024,4096]{1,0:T(8,128)(2,1)}, u32[]{:S(2)}) copy-start(bf16[1024,4096]{1,0:T(8,128)(2,1)} %all-gather.2.cloned.1.call-done) | copy-start | bytes 25165828
  158.1 8.0 %copy-start.4 = (bf16[1,4096,384]{2,1,0:T(8,128)(2,1)S(1)}, bf16[1,4096,384]{2,1,0:T(8,128)(2,1)}, u32[]{:S(2)}) copy-start(bf16[1,4096,384]{2,1,0:T(8,128)(2,1)} %param.22) | copy-start | bytes 9437188
  177.4 0.9 copy-start.5
  406.1 8.5 %all-to-all-start.2 = ((bf16[4,8,4096]{2,1,0:T(8,128)(2,1)}), bf16[4,8,4096]{2,1,0:T(8,128)(2,1)S(1)}, u32[]{:S(2)}, u32[]{:S(2)}) async-start(bf16[4,8,4096]{2,1,0:T(8,128)(2,1)} %bitcast.42), calls=%async_computation.3 | async-start | bytes 524288 | tf_op jit(solution)/shard_map/all_to_all | solution.py:269
Sparse Core Ops, SparseCore 0:
  62.2 95.8 all-gather.1
  177.5 228.5 reduce-scatter.1

commit v2 on v1

--- a/solution.py
+++ b/solution.py
@@ -217,58 +217,423 @@
     )(decay, x, b, c, skip_row, residual, ids_rows)
 
 
+SPLIT = 1664
+P_PART = (0, 768, SPLIT)
+Q_PART = (SPLIT, SPLIT + 1152, 4096)
+HALF = NZ // 2
+
+
+def expert_kernel(
+    mixed_ref, picked_ref, ids_rows_ref, ids_ref, residual_ref, gain_ref, router_ref,
+    gate_hbm, up_hbm, down_hbm,
+    out_ref,
+    gate_w, up_w, down_w, m_send, g_in, t_in, held, part, hidden, gated, lifted,
+    pz_in, py_in, qy_in, qz_in, ret_send, ret_in, stream, gate_col, stream16, result,
+    load_sems, send_sems, recv_sems,
+):
+    me = lax.axis_index("seq")
+    mx = lax.axis_index("exp")
+    z = me // NY
+    y = me % NY
+    d_model = residual_ref.shape[1]
+    d_part = d_model // NX
+
+    loads = [
+        pltpu.make_async_copy(src.at[0], dst, load_sems.at[i])
+        for i, (src, dst) in enumerate(((gate_hbm, gate_w), (up_hbm, up_w), (down_hbm, down_w)))
+    ]
+    for load in loads:
+        load.start()
+
+    ahead_z = {"seq": (z + 1) % NZ * NY + y}
+    behind_z = {"seq": (z + NZ - 1) % NZ * NY + y}
+    ahead_y = {"seq": z * NY + (y + 1) % NY}
+    behind_y = {"seq": z * NY + (y + NY - 1) % NY}
+    to_z = {1: ahead_z, -1: behind_z}
+    to_y = {1: ahead_y, -1: behind_y}
+
+    barrier = pltpu.get_barrier_semaphore()
+    for neighbour in (ahead_z, behind_z, ahead_y, behind_y):
+        pl.semaphore_signal(barrier, inc=1, device_id=neighbour, device_id_type=MESH)
+    for d in range(1, NX):
+        pl.semaphore_signal(barrier, inc=1, device_id={"exp": (mx + d) % NX}, device_id_type=MESH)
+
+    copies = {}
+
+    def send(key, src, dst, device):
+        i = len(copies)
+        copy = pltpu.make_async_remote_copy(
+            src_ref=src, dst_ref=dst, send_sem=send_sems.at[i], recv_sem=recv_sems.at[i],
+            device_id=device, device_id_type=MESH,
+        )
+        copies[key] = copy
+        copy.start()
+
+    def arrived(key):
+        copies[key].wait_recv()
+
+    offset = jnp.zeros((NX * RUN_CAP, 1), F32)
+    slot = (iota((NX * RUN_CAP, ROWS), 0) % RUN_CAP).astype(F32)
+    rows = jnp.zeros((NX * RUN_CAP, d_part), F32)
+    pack_slot = iota((RUN_CAP, NX * CAP), 0)
+    pack_block = iota((RUN_CAP, NX * CAP), 1) // CAP
+    pack_place = iota((RUN_CAP, NX * CAP), 1) % CAP
+    back_slot = iota((NX * CAP, RUN_CAP), 1)
+    back_block = iota((NX * CAP, RUN_CAP), 0) // CAP
+    back_place = iota((NX * CAP, RUN_CAP), 0) % CAP
+    pack = jnp.zeros((RUN_CAP, NX * CAP), F32)
+    back = jnp.zeros((NX * CAP, RUN_CAP), F32)
+    mine = jnp.zeros((1, 1), F32)
+    for b in range(NX):
+        first_row = ids_rows_ref[b][0:1, :ROWS]
+        member, rank, count = block_select(first_row, NX, RUN_CAP)
+        select = jnp.where(rank + offset == slot, member, 0.0).astype(BF16)
+        rows += jnp.dot(select, mixed_ref[ROWS * b : ROWS * b + ROWS, :], preferred_element_type=F32)
+        offset += count
+        here = jnp.sum((first_row == mx).astype(F32), axis=1, keepdims=True)
+
+        def match(of_block, of_place, of_slot):
+            place = of_place.astype(F32)
+            hit = (of_block == b) & (place < here) & (place + mine == of_slot.astype(F32))
+            return hit.astype(F32)
+
+        pack += match(pack_block, pack_place, pack_slot)
+        back += match(back_block, back_place, back_slot)
+        mine += here
+    m_send[...] = rows.astype(BF16).reshape(NX, RUN_CAP, d_part)
+
+    pl.semaphore_wait(barrier, 4 + NX - 1)
+    for d in range(1, NX):
+        to = (mx + d) % NX
+        send(("row", d), m_send.at[to], g_in.at[mx], {"exp": to})
+    for d in range(1, NX):
+        to = (mx + d) % NX
+        start_row = pl.multiple_of(to * ROWS, ROWS)
+        send(("token", d), mixed_ref.at[pl.ds(start_row, ROWS), :], t_in.at[mx], {"exp": to})
+    g_in[mx] = m_send[mx]
+    t_in[mx] = mixed_ref[pl.ds(pl.multiple_of(mx * ROWS, ROWS), ROWS), :]
+
+    gain = gain_ref[...]
+
+    def normalize(wide):
+        return (wide * lax.rsqrt(jnp.mean(wide * wide, axis=-1, keepdims=True) + 1e-06) * gain).astype(BF16)
+
+    stream16[...] = jnp.dot(pack.astype(BF16), picked_ref[...], preferred_element_type=F32)
+    for d in range(1, NX):
+        arrived(("row", d))
+    for i in range(NX):
+        cols = slice(d_part * i, d_part * i + d_part)
+        stream16[:, cols] = (stream16[:, cols] + g_in[i].astype(F32)).astype(BF16).astype(F32)
+    held[z, y] = normalize(stream16[...])
+
+    whole_p = pl.ds(P_PART[0], P_PART[2] - P_PART[0])
+    whole_q = pl.ds(Q_PART[0], Q_PART[2] - Q_PART[0])
+    p_cols = (pl.ds(P_PART[0], P_PART[1] - P_PART[0]), pl.ds(P_PART[1], P_PART[2] - P_PART[1]))
+    q_cols = (pl.ds(Q_PART[0], Q_PART[1] - Q_PART[0]), pl.ds(Q_PART[1], Q_PART[2] - Q_PART[1]))
+
+    def far(way):
+        return 0 if way == 1 else 1
+
+    def pieces(way, distance, last):
+        if distance == last:
+            return (far(way),)
+        return (far(way), 1 - far(way))
+
+    def at_z(shift):
+        return (z + shift + NZ) % NZ
+
+    def at_y(shift):
+        return (y + shift + NY) % NY
+
+    def planes_of(distance):
+        if distance == 0:
+            return (0,)
+        if distance == HALF:
+            return (HALF,)
+        return (-distance, distance)
+
+    def share(key, ref, device):
+        send(key, ref, ref, device)
+
+    def q_round_y(plane):
+        for way in (1, -1):
+            share(("qy", plane, 1, way), held.at[at_z(plane), y, :, whole_q], to_y[way])
+
+    def q_relay_y(plane):
+        for way in (1, -1):
+            arrived(("qy", plane, 1, way))
+            share(("qy", plane, 2, way), held.at[at_z(plane), at_y(-way), :, q_cols[far(way)]], to_y[way])
+
+    for way in (1, -1):
+        share(("py", 1, way), held.at[z, y, :, whole_p], to_y[way])
+        for piece in pieces(way, 1, HALF):
+            share(("qz", 1, way, piece), held.at[z, y, :, q_cols[piece]], to_z[way])
+    q_round_y(0)
+    for way in (1, -1):
+        arrived(("py", 1, way))
+        share(("py", 2, way), held.at[z, at_y(-way), :, p_cols[far(way)]], to_y[way])
+    q_relay_y(0)
+    for way in (1, -1):
+        arrived(("py", 2, way))
+    for way in (1, -1):
+        for piece in pieces(way, 1, HALF):
+            share(("pz", 1, way, piece), held.at[z, :, :, p_cols[piece]], to_z[way])
+
+    def own_tokens():
+        for d in range(1, NX):
+            arrived(("token", d))
+        for i in range(NX):
+            cols = slice(d_part * i, d_part * i + d_part)
+            stream[:, cols] = (residual_ref[:, cols].astype(F32) + t_in[i].astype(F32)).astype(BF16)
+        normed = normalize(stream[...].astype(F32))
+        logits = jnp.dot(normed, router_ref[...], preferred_element_type=F32)
+        experts = iota(logits.shape, 1)
+        picks = [
+            jnp.sum(jnp.where(experts == ids_ref[:, j : j + 1], logits, 0.0), axis=-1, keepdims=True)
+            for j in range(2)
+        ]
+        gate_col[...] = jnp.broadcast_to(jax.nn.sigmoid(picks[0] - picks[1]), gate_col.shape)
+
+    step_k = 512
+
+    def compute(planes):
+        for plane in planes:
+            for way in (1, -1):
+                arrived(("qy", plane, 2, way))
+        count = len(planes) * NY * RUN_CAP
+        gated[:count] = jnp.zeros((count, gated.shape[1]), F32)
+        lifted[:count] = jnp.zeros((count, lifted.shape[1]), F32)
+
+        def up_step(k, carry):
+            depth = pl.ds(pl.multiple_of(k * step_k, step_k), step_k)
+            blocks = [held[at_z(plane), :, :, depth].reshape(NY * RUN_CAP, step_k) for plane in planes]
+            tokens = blocks[0] if len(blocks) == 1 else jnp.concatenate(blocks, axis=0)
+            gated[:count] += jnp.dot(tokens, gate_w[depth, :], preferred_element_type=F32)
+            lifted[:count] += jnp.dot(tokens, up_w[depth, :], preferred_element_type=F32)
+            return carry
+
+        lax.fori_loop(0, d_model // step_k, up_step, 0)
+        hidden[:count] = (jax.nn.silu(gated[:count]) * lifted[:count]).astype(BF16)
+
+        def down_step(n, carry):
+            cols = pl.ds(pl.multiple_of(n * step_k, step_k), step_k)
+            sums = jnp.dot(hidden[:count], down_w[:, cols], preferred_element_type=F32).astype(BF16)
+            for i, plane in enumerate(planes):
+                rows_of = sums[i * NY * RUN_CAP : (i + 1) * NY * RUN_CAP]
+                part[at_z(plane), :, :, cols] = rows_of.reshape(NY, RUN_CAP, step_k)
+            return carry
+
+        lax.fori_loop(0, d_model // step_k, down_step, 0)
+
+    for distance in range(1, HALF + 1):
+        for way in (1, -1):
+            for piece in pieces(way, distance, HALF):
+                arrived(("qz", distance, way, piece))
+                if distance < HALF and piece in pieces(way, distance + 1, HALF):
+                    share(
+                        ("qz", distance + 1, way, piece),
+                        held.at[at_z(-way * distance), y, :, q_cols[piece]], to_z[way],
+                    )
+        for plane in planes_of(distance):
+            q_round_y(plane)
+        for way in (1, -1):
+            for piece in pieces(way, distance, HALF):
+                arrived(("pz", distance, way, piece))
+                if distance < HALF and piece in pieces(way, distance + 1, HALF):
+                    share(
+                        ("pz", distance + 1, way, piece),
+                        held.at[at_z(-way * distance), :, :, p_cols[piece]], to_z[way],
+                    )
+        for plane in planes_of(distance):
+            q_relay_y(plane)
+        if distance == 1:
+            own_tokens()
+            for load in loads:
+                load.wait()
+        compute(planes_of(distance - 1))
+
+    def add(where, piece_in):
+        total = part[where].astype(F32) + piece_in.astype(F32)
+        part[where] = total.astype(BF16)
+
+    def q_sum_start(plane):
+        for way in (1, -1):
+            cols = q_cols[far(way)]
+            send(
+                ("rqy", plane, 2, way), part.at[at_z(plane), at_y(2 * way), :, cols],
+                qy_in.at[plane + HALF - 1, far(way), 1, :, pl.ds(cols.start - SPLIT, cols.size)], to_y[way],
+            )
+
+    def q_sum_relay(plane):
+        for way in (1, -1):
+            cols = q_cols[far(way)]
+            arrived(("rqy", plane, 2, way))
+            add(
+                (at_z(plane), at_y(way), slice(None), cols),
+                qy_in[plane + HALF - 1, far(way), 1, :, pl.ds(cols.start - SPLIT, cols.size)],
+            )
+            send(
+                ("rqy", plane, 1, way), part.at[at_z(plane), at_y(way), :, whole_q],
+                qy_in.at[plane + HALF - 1, far(way), 0], to_y[way],
+            )
+
+    def q_sum_y(plane):
+        for way in (1, -1):
+            arrived(("rqy", plane, 1, way))
+        total = part[at_z(plane), y, :, whole_q].astype(F32)
+        total += qy_in[plane + HALF - 1, 0, 0].astype(F32) + qy_in[plane + HALF - 1, 1, 0].astype(F32)
+        return total
+
+    def p_send(distance):
+        for way in (1, -1):
+            for piece in pieces(way, distance, HALF):
+                cols = p_cols[piece]
+                if distance < HALF and piece in pieces(way, distance + 1, HALF):
+                    arrived(("rpz", distance + 1, way, piece))
+                    add((at_z(way * distance), slice(None), slice(None), cols), pz_in[far(way), distance, :, :, cols])
+                send(
+                    ("rpz", distance, way, piece), part.at[at_z(way * distance), :, :, cols],
+                    pz_in.at[far(way), distance - 1, :, :, cols], to_z[way],
+                )
+
+    def q_send(distance):
+        for plane in planes_of(distance):
+            part[at_z(plane), y, :, whole_q] = q_sum_y(plane).astype(BF16)
+        for way in (1, -1):
+            for piece in pieces(way, distance, HALF):
+                cols = q_cols[piece]
+                inner = pl.ds(cols.start - SPLIT, cols.size)
+                if distance < HALF and piece in pieces(way, distance + 1, HALF):
+                    arrived(("rqz", distance + 1, way, piece))
+                    add((at_z(way * distance), y, slice(None), cols), qz_in[far(way), distance, :, inner])
+                send(
+                    ("rqz", distance, way, piece), part.at[at_z(way * distance), y, :, cols],
+                    qz_in.at[far(way), distance - 1, :, inner], to_z[way],
+                )
+
+    for distance in range(HALF - 1, -1, -1):
+        for plane in planes_of(distance):
+            q_sum_start(plane)
+    compute(planes_of(HALF))
+    for plane in planes_of(HALF):
+        q_sum_start(plane)
+    p_send(HALF)
+    for distance in range(HALF, -1, -1):
+        for plane in planes_of(distance):
+            q_sum_relay(plane)
+    q_send(HALF)
+    for distance in range(HALF - 1, 0, -1):
+        p_send(distance)
+        q_send(distance)
+
+    for way in (1, -1):
+        for piece in pieces(way, 1, HALF):
+            arrived(("rpz", 1, way, piece))
+    sums = part[z, :, :, whole_p].astype(F32) + pz_in[0, 0].astype(F32) + pz_in[1, 0].astype(F32)
+    part[z, :, :, whole_p] = sums.astype(BF16)
+    for way in (1, -1):
+        cols = p_cols[far(way)]
+        send(("rpy", 2, way), part.at[z, at_y(2 * way), :, cols], py_in.at[far(way), 1, :, cols], to_y[way])
+
+    def give_back(cols, name):
+        give = jnp.dot(back.astype(BF16), result[:, cols], preferred_element_type=F32)
+        ret_send[:, :, cols] = give.astype(BF16).reshape(NX, CAP, cols.size)
+        for d in range(1, NX):
+            to = (mx + d) % NX
+            send((name, d), ret_send.at[to, :, cols], ret_in.at[mx, :, cols], {"exp": to})
+        ret_in[mx, :, cols] = ret_send[mx, :, cols]
+
+    total = q_sum_y(0)
+    for way in (1, -1):
+        arrived(("rpy", 2, way))
+        cols = p_cols[far(way)]
+        add((z, at_y(way), slice(None), cols), py_in[far(way), 1, :, cols])
+        send(("rpy", 1, way), part.at[z, at_y(way), :, whole_p], py_in.at[far(way), 0], to_y[way])
+    for way in (1, -1):
+        for piece in pieces(way, 1, HALF):
+            arrived(("rqz", 1, way, piece))
+    total += qz_in[0, 0].astype(F32) + qz_in[1, 0].astype(F32)
+    result[:, whole_q] = total.astype(BF16)
+    give_back(whole_q, "back_q")
+    for way in (1, -1):
+        arrived(("rpy", 1, way))
+    total = part[z, y, :, whole_p].astype(F32) + py_in[0, 0].astype(F32) + py_in[1, 0].astype(F32)
+    result[:, whole_p] = total.astype(BF16)
+    give_back(whole_p, "back_p")
+
+    own_expert = iota((ROWS, NX * CAP), 1) // CAP
+    own_slot = iota((ROWS, NX * CAP), 1) % CAP
+    member = (ids_ref[:, 0:1] == own_expert).astype(F32)
+    before = (iota((ROWS, ROWS), 1) < iota((ROWS, ROWS), 0)).astype(BF16)
+    rank = jnp.dot(before, member.astype(BF16), preferred_element_type=F32)
+    select = jnp.where(rank == own_slot.astype(F32), member, 0.0).astype(BF16)
+    for name, cols in (("back_q", whole_q), ("back_p", whole_p)):
+        for d in range(1, NX):
+            arrived((name, d))
+        combined = jnp.dot(select, ret_in[:, :, cols].reshape(NX * CAP, cols.size), preferred_element_type=F32)
+        out_ref[:, cols] = (stream[:, cols].astype(F32) + gate_col[:, 0:1] * combined).astype(BF16)
+    for copy in copies.values():
+        copy.wait_send()
+
+
+def experts(mixed, picked, ids_rows, ids, residual, gain, router, gate_weight, up_weight, down_weight):
+    rows, d = residual.shape
+    units = gate_weight.shape[2]
+    d_part = mixed.shape[1]
+    vmem = pl.BlockSpec(memory_space=pltpu.VMEM)
+    hbm = pl.BlockSpec(memory_space=pl.ANY)
+    p_width, q_width = SPLIT, d - SPLIT
+    return pl.pallas_call(
+        expert_kernel,
+        out_shape=jax.ShapeDtypeStruct((rows, d), BF16),
+        in_specs=[vmem] * 7 + [hbm] * 3,
+        out_specs=vmem,
+        scratch_shapes=[
+            pltpu.VMEM((d, units), BF16),
+            pltpu.VMEM((d, units), BF16),
+            pltpu.VMEM((units, d), BF16),
+            pltpu.VMEM((NX, RUN_CAP, d_part), BF16),
+            pltpu.VMEM((NX, RUN_CAP, d_part), BF16),
+            pltpu.VMEM((NX, ROWS, d_part), BF16),
+            pltpu.VMEM((NZ, NY, RUN_CAP, d), BF16),
+            pltpu.VMEM((NZ, NY, RUN_CAP, d), BF16),
+            pltpu.VMEM((2 * NY * RUN_CAP, units), BF16),
+            pltpu.VMEM((2 * NY * RUN_CAP, units), F32),
+            pltpu.VMEM((2 * NY * RUN_CAP, units), F32),
+            pltpu.VMEM((2, HALF, NY, RUN_CAP, p_width), BF16),
+            pltpu.VMEM((2, 2, RUN_CAP, p_width), BF16),
+            pltpu.VMEM((NZ, 2, 2, RUN_CAP, q_width), BF16),
+            pltpu.VMEM((2, HALF, RUN_CAP, q_width), BF16),
+            pltpu.VMEM((NX, CAP, d), BF16),
+            pltpu.VMEM((NX, CAP, d), BF16),
+            pltpu.VMEM((rows, d), BF16),
+            pltpu.VMEM((rows, 128), F32),
+            pltpu.VMEM((RUN_CAP, d), F32),
+            pltpu.VMEM((RUN_CAP, d), BF16),
+            pltpu.SemaphoreType.DMA((3,)),
+            pltpu.SemaphoreType.DMA((160,)),
+            pltpu.SemaphoreType.DMA((160,)),
+        ],
+        compiler_params=pltpu.CompilerParams(
+            collective_id=1, has_side_effects=True, vmem_limit_bytes=60 * 1024 * 1024
+        ),
+        name="experts",
+    )(mixed, picked, ids_rows, ids, residual, gain, router, gate_weight, up_weight, down_weight)
+
+
 def body(
     head_inputs, input_matrix, output_matrix, log_decay, skip_gain, residual, norm_gain,
     router_weight, expert_ids, gate_weight, up_weight, down_weight,
 ):
     skip_row = jnp.repeat(skip_gain, P_SIZE)[None, :]
     ids_rows = jnp.pad(expert_ids.T, ((0, 6), (0, 64)), constant_values=99)
-    mamba_out, picked, ids_all = mamba(
+    mixed, picked, ids_all = mamba(
         head_inputs, input_matrix, output_matrix, log_decay, skip_row, residual, ids_rows
     )
-    token_rows = lax.all_to_all(mamba_out, "exp", split_axis=0, concat_axis=1, tiled=True)
-    stream = (residual.astype(jnp.float32) + token_rows.astype(jnp.float32)).astype(jnp.bfloat16)
-    stream_wide = stream.astype(jnp.float32)
-    normed = (
-        stream_wide
-        * lax.rsqrt(jnp.mean(stream_wide * stream_wide, axis=-1, keepdims=True) + 1e-06)
-        * norm_gain
-    ).astype(jnp.bfloat16)
-    logits = jnp.dot(normed, router_weight, preferred_element_type=jnp.float32)
-    expert_iota = lax.broadcasted_iota(jnp.int32, logits.shape, 1)
-    first = expert_ids[:, 0]
-    second = expert_ids[:, 1]
-    first_logit = jnp.sum(jnp.where(expert_iota == first[:, None], logits, 0.0), axis=-1)
-    second_logit = jnp.sum(jnp.where(expert_iota == second[:, None], logits, 0.0), axis=-1)
-    gate = jax.nn.sigmoid(first_logit - second_logit)
-    flight = lax.axis_size("exp")
-    member = (first[:, None] == jnp.arange(flight, dtype=jnp.int32)[None, :]).astype(jnp.int32)
-    ranking = jnp.cumsum(member, axis=0) - member
-    slots = jnp.sum(ranking * member, axis=-1)
-    chosen = (member.T[:, None, :] == 1) & (
-        slots[None, None, :] == jnp.arange(CAP, dtype=jnp.int32)[None, :, None]
+    return experts(
+        mixed, picked, ids_all, expert_ids, residual, norm_gain[None, :], router_weight,
+        gate_weight, up_weight, down_weight,
     )
-    select = chosen.astype(jnp.bfloat16)
-    outbound = jnp.einsum("ecr,rd->ecd", select, normed, preferred_element_type=jnp.float32).astype(
-        jnp.bfloat16
-    )
-    model_width = outbound.shape[2]
-    inbound = lax.all_to_all(outbound, "exp", split_axis=0, concat_axis=0, tiled=True)
-    routed = inbound.reshape(flight * CAP, model_width)
-    fragment = lax.all_gather(routed, "seq", axis=0, tiled=True)
-    gated = jnp.dot(fragment, gate_weight[0], preferred_element_type=jnp.float32)
-    lifted = jnp.dot(fragment, up_weight[0], preferred_element_type=jnp.float32)
-    hidden_all = (jax.nn.silu(gated) * lifted).astype(jnp.bfloat16)
-    summed = lax.psum_scatter(
-        jnp.dot(hidden_all, down_weight[0], preferred_element_type=jnp.float32).astype(jnp.bfloat16),
-        "seq",
-        scatter_dimension=0,
-        tiled=True,
-    )
-    expert_out = summed.reshape(flight, CAP, model_width)
-    returned = lax.all_to_all(expert_out, "exp", split_axis=0, concat_axis=0, tiled=True)
-    combined = jnp.einsum("ecr,ecd->rd", select, returned, preferred_element_type=jnp.float32)
-    return (stream_wide + gate[:, None] * combined).astype(jnp.bfloat16)
 
 
 def solution(mesh):

time: 426 us -> 137 us (0.32)
  waiting for transfers between devices: 331 us -> 0 us
  Pallas kernels: 29 us -> 129 us
  matrix products: 23.1 us -> 0 us
  between operations: 13.5 us -> 0.02 us
  blocking collectives: 9.99 us -> 0 us
  starting transfers between devices: 9.65 us -> 0 us
    reduce_scatter x1 -> x0, waiting for transfers between devices: 226 us -> none  [body(): lax.psum_scatter(jnp.dot(hidden_all, down_weight[0], preferred_element_ty...]
    pallas_call x0 -> x1, Pallas kernels: none -> 99.9 us  [experts(): pl.pallas_call(expert_kernel, out_shape=jax.ShapeDtypeStruct((rows, d), B...]
    all_gather x1 -> x0, waiting for transfers between devices: 96 us -> none  [body(): fragment = lax.all_gather(routed, 'seq', axis=0, tiled=True)]
    dot_general x6 -> x0, matrix products: 23.1 us -> none  [the longest x1 7.97 us: body(): jnp.dot(fragment, gate_weight[0], preferred_element_type=jnp.float32)]
    all_to_all x1 -> x0, blocking collectives: 9.99 us -> none  [body(): lax.all_to_all(outbound, 'exp', split_axis=0, concat_axis=0, tiled=True)]
    all_to_all x2 -> x0, starting transfers between devices: 9.61 us -> none  [the longest x1 4.81 us: body(): lax.all_to_all(mamba_out, 'exp', split_axis=0, concat_axis=1, tiled=True)]
    all_to_all x2 -> x0, waiting for transfers between devices: 8.79 us -> none  [the longest x1 5.09 us: body(): lax.all_to_all(mamba_out, 'exp', split_axis=0, concat_axis=1, tiled=True)]
  transfers between devices with their start and end apart: 4 -> 0, of which waited for: 4 -> 0; matrix products, arithmetic and copies ran while one was open for 1% -> 0% of each run, Pallas kernels for 0% -> 0%
where the time goes in v2:
time: 137 us
  Pallas kernels  129 us (94%)
  local copies, waits for them, and re-layouts  8.16 us (6%)
    pallas_call x1, Pallas kernels, experts(): pl.pallas_call(expert_kernel, out_shape=jax.ShapeDtypeStruct((rows, d), B...  99.9 us
    pallas_call x1, Pallas kernels, mamba(): pl.pallas_call(mamba_kernel, out_shape=(jax.ShapeDtypeStruct((length, wid...  29.1 us
    unnamed x3, local copies, waits for them, and re-layouts  5.49 us

profile of v2, /device:TPU:4, one launch (start us, length us, event | category | flops | bytes accessed | tf_op | source)
XLA Modules:
  0.0 137.1 jit_solution(12961580433778230877)
XLA Ops:
  0.0 1.3 pad.4.ids_ref
  1.3 0.7 broadcast_in_dim.6
  2.0 0.7 broadcast_in_dim_reshape.3.skip_ref
  2.7 1.4 %copy.13.ids_ref = s32[64,2]{1,0:T(8,128)} copy(s32[64,2]{0,1:T(2,128)} %param.20) | data formatting | bytes 1024 | tf_op args[8]
  4.1 29.1 %mamba.1 = (bf16[256,1024]{1,0:T(8,128)(2,1)}, bf16[32,4096]{1,0:T(8,128)(2,1)}, s32[4,8,128]{2,1,0:T(8,128)}) custom-call(f32[16,256]{1,0:T(8,128)} %decay_ref.1, bf16[256,1024]{1,0:T(8,128)(2,1)} %x_ref.1, bf16[256,128]{1,0:T(8,128)(2,1)} %b_ref.1, bf16[256,128]{1,0:T(8,128)(2,1)} %c_ref.1, f32[1,1024]{1,0:T(1,128)} %broadcast_in_dim_reshape.3.skip_ref, ...), custom_call_target="tpu_custom_call" | custom-call | tf_op jit(solution)/shard_map/mamba/pallas_call | solution.py:191
  33.1 2.2 %copy.14.router_ref = bf16[4096,16]{1,0:T(8,128)(2,1)} copy(bf16[4096,16]{0,1:T(8,128)(2,1)} %param.19) | data formatting | bytes 262144 | tf_op args[7]
  35.4 99.9 %experts.1 = bf16[64,4096]{1,0:T(8,128)(2,1)} custom-call(bf16[256,1024]{1,0:T(8,128)(2,1)} %get-tuple-element.8.mixed_ref, bf16[32,4096]{1,0:T(8,128)(2,1)} %get-tuple-element.9.picked_ref, s32[4,8,128]{2,1,0:T(8,128)} %get-tuple-element.10.ids_rows_ref, s32[64,2]{1,0:T(8,128)} %copy.13.ids_ref, bf16[64,4096]{1,0:T(8,128)(2,1)} %residual_ref.3, ...), custom_call_target="tpu_custom_call" | custom-call | tf_op jit(solution)/shard_map/experts/pallas_call | solution.py:586
  135.2 1.9 %copy.16 = bf16[64,4096]{1,0:T(8,128)(2,1)} copy(bf16[64,4096]{1,0:T(8,128)(2,1)} %experts.1) | data formatting | bytes 1048576

commit v3 on v2

--- a/solution.py
+++ b/solution.py
@@ -108,7 +108,7 @@
     dec_recv[me] = dec_send[me // 2]
 
     ids = ids_ref[...]
-    member, rank, _ = block_select(ids[0:1, :ROWS], NX, CAP)
+    member, rank, _ = block_select(ids[0:1, :], NX, CAP)
     slot = (iota((NX * CAP, ROWS), 0) % CAP).astype(F32)
     select = jnp.where(rank == slot, member, 0.0).astype(BF16)
     rows = jnp.dot(select, residual_ref[...], preferred_element_type=F32)
@@ -138,7 +138,8 @@
             mixing = (jnp.exp(gap) * scores).astype(BF16)
             parts.append(jnp.dot(mixing, x_pair, preferred_element_type=F32))
         own = jnp.where(left, parts[0], parts[1])
-        acc[:, pair] = own + skip_ref[:, pair] * x_pair.astype(F32)
+        gains = [jnp.broadcast_to(skip_ref[:, h : h + 1], (1, 2 * P_SIZE)) for h in (2 * i, 2 * i + 1)]
+        acc[:, pair] = own + jnp.where(left[0:1], gains[0], gains[1]) * x_pair.astype(F32)
         grow[:, pair] = spread(grown, i)
 
     def drain(ref, sem):
@@ -193,7 +194,7 @@
         out_shape=(
             jax.ShapeDtypeStruct((length, width), BF16),
             jax.ShapeDtypeStruct((NX * CAP, d), BF16),
-            jax.ShapeDtypeStruct((NX, 8, 128), jnp.int32),
+            jax.ShapeDtypeStruct((NX, 2, ROWS), jnp.int32),
         ),
         in_specs=[vmem] * 7,
         out_specs=(vmem, vmem, vmem),
@@ -208,7 +209,7 @@
             pltpu.VMEM((length, width), F32),
             pltpu.VMEM((NX, CAP, d), BF16),
             pltpu.VMEM((NX, CAP, d), BF16),
-            pltpu.VMEM((NX, 8, 128), jnp.int32),
+            pltpu.VMEM((NX, 2, ROWS), jnp.int32),
             pltpu.SemaphoreType.DMA((8,)),
             pltpu.SemaphoreType.DMA((2,)),
         ],
@@ -285,7 +286,7 @@
     back = jnp.zeros((NX * CAP, RUN_CAP), F32)
     mine = jnp.zeros((1, 1), F32)
     for b in range(NX):
-        first_row = ids_rows_ref[b][0:1, :ROWS]
+        first_row = ids_rows_ref[b][0:1, :]
         member, rank, count = block_select(first_row, NX, RUN_CAP)
         select = jnp.where(rank + offset == slot, member, 0.0).astype(BF16)
         rows += jnp.dot(select, mixed_ref[ROWS * b : ROWS * b + ROWS, :], preferred_element_type=F32)
@@ -314,6 +315,10 @@
     t_in[mx] = mixed_ref[pl.ds(pl.multiple_of(mx * ROWS, ROWS), ROWS), :]
 
     gain = gain_ref[...]
+    same = (iota((ROWS, ROWS), 0) == iota((ROWS, ROWS), 1)).astype(BF16)
+    ids_cols = lax.dot_general(
+        same, ids_ref[...].astype(F32).astype(BF16), CONTRACT_COLS, preferred_element_type=F32
+    )
 
     def normalize(wide):
         return (wide * lax.rsqrt(jnp.mean(wide * wide, axis=-1, keepdims=True) + 1e-06) * gain).astype(BF16)
@@ -386,10 +391,10 @@
             cols = slice(d_part * i, d_part * i + d_part)
             stream[:, cols] = (residual_ref[:, cols].astype(F32) + t_in[i].astype(F32)).astype(BF16)
         normed = normalize(stream[...].astype(F32))
-        logits = jnp.dot(normed, router_ref[...], preferred_element_type=F32)
-        experts = iota(logits.shape, 1)
+        logits = lax.dot_general(normed, router_ref[...], CONTRACT_COLS, preferred_element_type=F32)
+        experts = iota(logits.shape, 1).astype(F32)
         picks = [
-            jnp.sum(jnp.where(experts == ids_ref[:, j : j + 1], logits, 0.0), axis=-1, keepdims=True)
+            jnp.sum(jnp.where(experts == ids_cols[:, j : j + 1], logits, 0.0), axis=-1, keepdims=True)
             for j in range(2)
         ]
         gate_col[...] = jnp.broadcast_to(jax.nn.sigmoid(picks[0] - picks[1]), gate_col.shape)
@@ -563,7 +568,7 @@
 
     own_expert = iota((ROWS, NX * CAP), 1) // CAP
     own_slot = iota((ROWS, NX * CAP), 1) % CAP
-    member = (ids_ref[:, 0:1] == own_expert).astype(F32)
+    member = (ids_cols[:, 0:1] == own_expert.astype(F32)).astype(F32)
     before = (iota((ROWS, ROWS), 1) < iota((ROWS, ROWS), 0)).astype(BF16)
     rank = jnp.dot(before, member.astype(BF16), preferred_element_type=F32)
     select = jnp.where(rank == own_slot.astype(F32), member, 0.0).astype(BF16)
@@ -625,13 +630,12 @@
     head_inputs, input_matrix, output_matrix, log_decay, skip_gain, residual, norm_gain,
     router_weight, expert_ids, gate_weight, up_weight, down_weight,
 ):
-    skip_row = jnp.repeat(skip_gain, P_SIZE)[None, :]
-    ids_rows = jnp.pad(expert_ids.T, ((0, 6), (0, 64)), constant_values=99)
+    ids = expert_ids.T
     mixed, picked, ids_all = mamba(
-        head_inputs, input_matrix, output_matrix, log_decay, skip_row, residual, ids_rows
+        head_inputs, input_matrix, output_matrix, log_decay, skip_gain[None, :], residual, ids
     )
     return experts(
-        mixed, picked, ids_all, expert_ids, residual, norm_gain[None, :], router_weight,
+        mixed, picked, ids_all, ids, residual, norm_gain[None, :], router_weight.T,
         gate_weight, up_weight, down_weight,
     )
 

time: 137 us -> 130 us (0.949)
  local copies, waits for them, and re-layouts: 8.16 us -> 1.87 us
    unnamed x3 -> x1, local copies, waits for them, and re-layouts: 5.49 us -> 1.87 us
where the time goes in v3:
time: 130 us
  Pallas kernels  128 us (98%)
  local copies, waits for them, and re-layouts  1.87 us (1%)
    pallas_call x1, Pallas kernels, experts(): pl.pallas_call(expert_kernel, out_shape=jax.ShapeDtypeStruct((rows, d), B...  99.4 us
    pallas_call x1, Pallas kernels, mamba(): pl.pallas_call(mamba_kernel, out_shape=(jax.ShapeDtypeStruct((length, wid...  28.9 us

profile of v3, /device:TPU:4, one launch (start us, length us, event | category | flops | bytes accessed | tf_op | source)
XLA Modules:
  0.0 130.2 jit_solution(17878066213974119222)
XLA Ops:
  0.0 28.9 %mamba.1 = (bf16[256,1024]{1,0:T(8,128)(2,1)}, bf16[32,4096]{1,0:T(8,128)(2,1)}, s32[4,2,64]{2,1,0:T(2,128)}) custom-call(f32[16,256]{1,0:T(8,128)} %decay_ref.1, bf16[256,1024]{1,0:T(8,128)(2,1)} %x_ref.1, bf16[256,128]{1,0:T(8,128)(2,1)} %b_ref.1, bf16[256,128]{1,0:T(8,128)(2,1)} %c_ref.1, f32[1,16]{1,0:T(1,128)} %bitcast.8, ...), custom_call_target="tpu_custom_call" | custom-call | tf_op jit(solution)/shard_map/mamba/pallas_call | solution.py:192
  29.0 99.4 %experts.1 = bf16[64,4096]{1,0:T(8,128)(2,1)} custom-call(bf16[256,1024]{1,0:T(8,128)(2,1)} %get-tuple-element.8.mixed_ref, bf16[32,4096]{1,0:T(8,128)(2,1)} %get-tuple-element.9.picked_ref, s32[4,2,64]{2,1,0:T(2,128)} %get-tuple-element.10.ids_rows_ref, s32[2,64]{1,0:T(2,128)} %bitcast.7, bf16[64,4096]{1,0:T(8,128)(2,1)} %residual_ref.3, ...), custom_call_target="tpu_custom_call" | custom-call | tf_op jit(solution)/shard_map/experts/pallas_call | solution.py:591
  128.4 1.9 %copy.14 = bf16[64,4096]{1,0:T(8,128)(2,1)} copy(bf16[64,4096]{1,0:T(8,128)(2,1)} %experts.1) | data formatting | bytes 1048576
